TPU v7x, 32 devices: a whole 2x2x4 slice. The times are simulated.
32 devices in a mesh: groups: 2 (over y), sec: 2 (over x), row: 4 (over z), col: 2 (over core).
Axes of the slice: x: 2, y: 2, z: 4, core: 2. Of those that a mesh axis runs over, the one named last changes fastest.
Arguments:
- factors: bfloat16 [4, 2048, 2048], P(('groups', 'sec'), 'row', 'col'), parts along dimension 0, may hold values from -0.125 to 0.125
- inverses: bfloat16 [4, 2048, 2048], P(('groups', 'sec'), 'row', 'col'), parts along dimension 0, may hold values from -1.4 to 1.4, as said below
- sigma_end: float32 [4096, 2048], P(('groups', 'row'), 'col'), parts along dimension 0, may hold values from -1 to 6, as said below
Outputs:
- variance: float32 [4, 2048, 2048], P(('groups', 'sec'), 'row', 'col'), parts along dimension 0
There are 2 independent parts, one for each index of `groups`. A program takes and returns all parts, laid end to end along the dimension named above; each array names one. Nothing has to cross between parts.
Inputs may be any that keep to these rules, and one draw needn't show every extreme that they name: inverses[t] is lower triangular; its diagonal entries lie in 0.6 to 1.4. sigma_end is symmetric with diagonal entries in 2.5 to 6.
All inputs are finite; a program needn't handle non-finite values.
Results may differ from a plain program's by a relative error of at most 0.011.
Values may be sent and summed in bfloat16 or wider, within the bound.
A program may use at most 64 MiB of HBM per device.

v0:
```python
import jax
import jax.numpy as jnp
from jax import lax
from jax.sharding import PartitionSpec as P


def partner(shard, axis, stride):
    return lax.ppermute(shard, axis, [(i, i ^ 1 << stride) for i in range(lax.axis_size(axis))])


def passed_along(value, axis, steps):
    count = lax.axis_size(axis)
    first, last = (max(0, -steps), min(count, count - steps))
    return lax.ppermute(value, axis, [(source, source + steps) for source in range(first, last)])


def local(factors, inverses, sigma_end):
    row_size = lax.axis_size("row")
    col_size = lax.axis_size("col")
    sec_size = lax.axis_size("sec")
    row_index = lax.axis_index("row")
    col_index = lax.axis_index("col")
    sec_index = lax.axis_index("sec")
    _, tile_rows, _ = factors.shape
    per_column = row_size // col_size
    offset = row_index % per_column * tile_rows
    owns_panel = col_index == row_index // per_column

    def gather(tile):
        return lax.all_gather(tile, "row", axis=0, tiled=True)

    def left_of(full):
        mine = lax.dynamic_slice_in_dim(full, offset, tile_rows, 1)
        return jnp.where(owns_panel, mine, partner(mine, "col", 0))

    def cross(left, full):
        return lax.dot_general(
            left, full, (((0,), (0,)), ((), ())), preferred_element_type=jnp.float32
        )

    current = sigma_end.astype(jnp.bfloat16)
    factor = gather(factors[0])
    state = gather(current)
    inverse = gather(inverses[0])
    factor_left = left_of(factor)
    diagonal = cross(left_of(inverse), inverse)
    result = None
    for segment in range(sec_size):
        half = cross(factor_left, state).astype(jnp.bfloat16)
        whole = lax.all_gather(half, "col", axis=1, tiled=True)
        block = diagonal + jnp.dot(whole, factor, preferred_element_type=jnp.float32)
        active = sec_index == sec_size - 1 - segment
        result = block if result is None else jnp.where(active, block, result)
        if segment < sec_size - 1:
            state = gather(passed_along(block.astype(jnp.bfloat16), "sec", -1))
    return result[None]


def solution(mesh):
    in_specs = (
        P(("groups", "sec"), "row", "col"),
        P(("groups", "sec"), "row", "col"),
        P(("groups", "row"), "col"),
    )
    out_specs = P(("groups", "sec"), "row", "col")
    return jax.shard_map(local, mesh=mesh, in_specs=in_specs, out_specs=out_specs, check_vma=False)
```

profile of v0, /device:TPU:0, one launch (start us, length us, event | category | flops | bytes accessed | tf_op | source)
XLA Modules:
  0.0 415.6 jit_solution(8728628893357089546)
XLA Ops:
  6.5 0.0 all-gather.19.cloned.1.call-start
  6.5 0.7 all-gather.19.cloned.1.call-update
  7.3 0.0 all-gather.17.cloned.1.call-start
  7.3 0.7 all-gather.17.cloned.1.call-update
  8.0 0.0 all-gather.9.cloned.1.call-start
  8.1 2.8 convert_element_type.12
  10.8 0.0 all-gather.9.cloned.1.call-update
  10.8 0.0 all-gather.11.cloned.1.call-start
  10.9 81.5 %all-gather.19.cloned.1.call-done = bf16[1,2048,1024]{2,1,0:T(8,128)(2,1)} async-done(((bf16[1,512,1024]{2,1,0:T(8,128)(2,1)}), bf16[1,2048,1024]{2,1,0:T(8,128)(2,1)}) %all-gather.19.cloned.1.call-update) | async-done | bytes 4194320 | tf_op jit(solution)/shard_map/all_gather | solution.py:30
  92.4 1.7 dynamic-slice_bitcast_fusion
  94.2 0.1 collective-permute-start.1
  94.3 79.1 %all-gather.17.cloned.1.call-done = bf16[1,2048,1024]{2,1,0:T(8,128)(2,1)} async-done(((bf16[1,512,1024]{2,1,0:T(8,128)(2,1)}), bf16[1,2048,1024]{2,1,0:T(8,128)(2,1)}) %all-gather.17.cloned.1.call-update) | async-done | bytes 4194320 | tf_op jit(solution)/shard_map/all_gather | solution.py:30
  173.3 3.0 dynamic-slice_bitcast_fusion.1
  176.4 0.0 collective-permute-start
  176.4 77.9 %all-gather.9.cloned.1.call-done = bf16[2048,1024]{1,0:T(8,128)(2,1)} async-done(((bf16[512,1024]{1,0:T(8,128)(2,1)}), bf16[2048,1024]{1,0:T(8,128)(2,1)}) %all-gather.9.cloned.1.call-update) | async-done | bytes 4194320 | tf_op jit(solution)/shard_map/all_gather | solution.py:30
  254.2 0.0 collective-permute-done.1
  254.2 5.6 %convolution_convert_fusion.1 = bf16[512,1024]{1,0:T(8,128)(2,1)} fusion(bf16[2048,1024]{1,0:T(8,128)(2,1)} %all-gather.9.cloned.1.call-done, bf16[2048,512]{1,0:T(8,128)(2,1)S(1)} %dynamic-slice_bitcast_fusion, bf16[2048,512]{1,0:T(8,128)(2,1)} %collective-permute-done.1, pred[]{:T(512)S(6)} %eq.9), kind=kOutput, calls=%fused_computation.14 | convolution fusion | flops 2149056512 | bytes 9437185 | tf_op jit(solution)/shard_map/dot_general | solution.py:37
  259.8 0.0 all-gather.11.cloned.1.call-update
  259.8 0.0 all-gather.13.cloned.1.call-start
  259.8 0.0 collective-permute-done
  259.9 6.6 %fusion.4 = f32[512,1024]{1,0:T(8,128)} fusion(bf16[1,2048,1024]{2,1,0:T(8,128)(2,1)} %all-gather.17.cloned.1.call-done, bf16[2048,512]{1,0:T(8,128)(2,1)} %dynamic-slice_bitcast_fusion.1, bf16[2048,512]{1,0:T(8,128)(2,1)} %collective-permute-done, pred[]{:T(512)S(6)} %eq.9), kind=kOutput, calls=%fused_computation.4 | convolution fusion | flops 2148532224 | bytes 10485761 | tf_op jit(solution)/shard_map/dot_general | solution.py:37
  266.4 3.2 all-gather.11.cloned.1.call-done
  269.7 7.1 %fusion.13 = (bf16[512,1024]{1,0:T(8,128)(2,1)S(1)}, f32[512,1024]{1,0:T(8,128)}) fusion(f32[512,1024]{1,0:T(8,128)} %fusion.4, bf16[512,2048]{1,0:T(8,128)(2,1)} %all-gather.11.cloned.1.call-done, bf16[1,2048,1024]{2,1,0:T(8,128)(2,1)} %all-gather.19.cloned.1.call-done), kind=kOutput, calls=%fused_computation.15 | convolution fusion | flops 2148532224 | bytes 11534336 | tf_op jit(solution)/shard_map/dot_general | solution.py:51
  276.8 1.3 collective-permute-start.2
  278.1 25.9 %collective-permute-done.2 = bf16[512,1024]{1,0:T(8,128)(2,1)S(1)} collective-permute-done((bf16[512,1024]{1,0:T(8,128)(2,1)S(1)}, bf16[512,1024]{1,0:T(8,128)(2,1)S(1)}, u32[]{:S(2)}, u32[]{:S(2)}) %collective-permute-start.2) | collective-permute-done | bytes 1048608 | tf_op jit(solution)/shard_map/ppermute | solution.py:14
  304.0 0.0 copy-start
  304.0 1.0 copy-done
  305.0 0.0 all-gather.13.cloned.1.call-update
  305.0 0.0 all-gather.15.cloned.1.call-start
  305.0 81.2 %all-gather.13.cloned.1.call-done = bf16[2048,1024]{1,0:T(8,128)(2,1)} async-done(((bf16[512,1024]{1,0:T(8,128)(2,1)}), bf16[2048,1024]{1,0:T(8,128)(2,1)}) %all-gather.13.cloned.1.call-update) | async-done | bytes 4194320 | tf_op jit(solution)/shard_map/all_gather | solution.py:30
  386.3 5.5 %convolution_convert_fusion = bf16[512,1024]{1,0:T(8,128)(2,1)} fusion(bf16[2048,1024]{1,0:T(8,128)(2,1)} %all-gather.13.cloned.1.call-done, bf16[2048,512]{1,0:T(8,128)(2,1)S(1)} %dynamic-slice_bitcast_fusion, bf16[2048,512]{1,0:T(8,128)(2,1)} %collective-permute-done.1, pred[]{:T(512)S(6)} %eq.9), kind=kOutput, calls=%fused_computation.13 | convolution fusion | flops 2149056512 | bytes 9437185 | tf_op jit(solution)/shard_map/dot_general | solution.py:37
  391.8 0.0 all-gather.15.cloned.1.call-update
  391.8 9.9 %all-gather.15.cloned.1.call-done = bf16[512,2048]{1,0:T(8,128)(2,1)} async-done(((bf16[512,1024]{1,0:T(8,128)(2,1)}), bf16[512,2048]{1,0:T(8,128)(2,1)}) %all-gather.15.cloned.1.call-update) | async-done | bytes 2097168 | tf_op jit(solution)/shard_map/all_gather | solution.py:50
  401.7 7.1 %select_bitcast_fusion = f32[1,512,1024]{2,1,0:T(8,128)} fusion(f32[512,1024]{1,0:T(8,128)} %get-tuple-element.6, f32[512,1024]{1,0:T(8,128)} %fusion.4, bf16[512,2048]{1,0:T(8,128)(2,1)} %all-gather.15.cloned.1.call-done, bf16[1,2048,1024]{2,1,0:T(8,128)(2,1)} %all-gather.19.cloned.1.call-done, pred[]{:T(512)S(6)} %eq.8), kind=kOutput, calls=%fused_computation.8 | convolution fusion | flops 2148532224 | bytes 12582913 | tf_op jit(solution)/shard_map/dot_general | solution.py:51
Async XLA Ops:
  6.5 85.9 %all-gather.19.cloned.1.call-start = ((), (), s32[]{:S(2)}) async-start(), calls=%async_computation.5 | async-start | bytes 5242880 | tf_op jit(solution)/shard_map/all_gather | solution.py:30
  7.3 166.1 %all-gather.17.cloned.1.call-start = ((), (), s32[]{:S(2)}) async-start(), calls=%async_computation.4 | async-start | bytes 5242880 | tf_op jit(solution)/shard_map/all_gather | solution.py:30
  8.0 246.2 %all-gather.9.cloned.1.call-start = ((), (), s32[]{:S(2)}) async-start(), calls=%async_computation | async-start | bytes 5242880 | tf_op jit(solution)/shard_map/all_gather | solution.py:30
  10.8 258.9 %all-gather.11.cloned.1.call-start = ((), (), s32[]{:S(2)}) async-start(), calls=%async_computation.1 | async-start | bytes 3145728 | tf_op jit(solution)/shard_map/all_gather | solution.py:50
  94.2 160.1 %collective-permute-start.1 = (bf16[2048,512]{1,0:T(8,128)(2,1)S(1)}, bf16[2048,512]{1,0:T(8,128)(2,1)}, u32[]{:S(2)}, u32[]{:S(2)}) collective-permute-start(bf16[2048,512]{1,0:T(8,128)(2,1)S(1)} %dynamic-slice_bitcast_fusion), channel_id=1, source_target_pairs={{0,1},{1,0},{2,3},{3,2},{4,5},{5,4},{6,7},{7,6},{8,9},{9,8},{10,11... | collective-permute-start | bytes 6291464 | tf_op jit(solution)/shard_map/ppermute | solution.py:8
  176.4 83.5 %collective-permute-start = (bf16[2048,512]{1,0:T(8,128)(2,1)}, bf16[2048,512]{1,0:T(8,128)(2,1)}, u32[]{:S(2)}, u32[]{:S(2)}) collective-permute-start(bf16[2048,512]{1,0:T(8,128)(2,1)} %dynamic-slice_bitcast_fusion.1), channel_id=1, source_target_pairs={{0,1},{1,0},{2,3},{3,2},{4,5},{5,4},{6,7},{7,6},{8,9},{9,8},{10,11... | collective-permute-start | bytes 6291464 | tf_op jit(solution)/shard_map/ppermute | solution.py:8
  259.8 126.5 %all-gather.13.cloned.1.call-start = ((), (), s32[]{:S(2)}) async-start(), calls=%async_computation.2 | async-start | bytes 5242880 | tf_op jit(solution)/shard_map/all_gather | solution.py:30
  276.8 27.2 %collective-permute-start.2 = (bf16[512,1024]{1,0:T(8,128)(2,1)S(1)}, bf16[512,1024]{1,0:T(8,128)(2,1)S(1)}, u32[]{:S(2)}, u32[]{:S(2)}) collective-permute-start(bf16[512,1024]{1,0:T(8,128)(2,1)S(1)} %get-tuple-element.5), channel_id=1, source_target_pairs={{8,0},{9,1},{10,2},{11,3},{12,4},{13,5},{14,6},{15,7},{24,16},{25,... | collective-permute-start | bytes 3145736 | tf_op jit(solution)/shard_map/ppermute | solution.py:14
  304.0 1.0 copy-start
  305.0 96.7 %all-gather.15.cloned.1.call-start = ((), (), s32[]{:S(2)}) async-start(), calls=%async_computation.3 | async-start | bytes 3145728 | tf_op jit(solution)/shard_map/all_gather | solution.py:50
Sparse Core Ops, SparseCore 0:
  8.9 83.4 all-gather.18
  94.0 79.2 all-gather.16
  174.9 79.2 all-gather.8
  259.9 9.7 all-gather.10
  305.1 81.1 all-gather.12
  391.9 9.7 all-gather.14
where the time goes:
time: 416 us
  waiting for transfers between devices  360 us (87%)
  matrix products  31.9 us (8%)
  between operations  13.5 us (3%)
  local copies, waits for them, and re-layouts  5.75 us (1%)
    all_gather x4, waiting for transfers between devices, gather(): return lax.all_gather(tile, 'row', axis=0, tiled=True)  320 us
    ppermute x1, waiting for transfers between devices, passed_along(): lax.ppermute(value, axis, [(source, source + steps) for source in range(f...  25.9 us
    dot_general x3, matrix products, cross(): lax.dot_general(left, full, (((0,), (0,)), ((), ())), preferred_element_t...  17.7 us
    dot_general x2, matrix products, local(): jnp.dot(whole, factor, preferred_element_type=jnp.float32)  14.2 us
    all_gather x2, waiting for transfers between devices, local(): whole = lax.all_gather(half, 'col', axis=1, tiled=True)  13.1 us
  transfers between devices with their start and end apart: 9, of which 7 were waited for; matrix products, arithmetic and copies ran while one was open for 5% of the time, Pallas kernels for 0%

commit v1 on v0

--- a/solution.py
+++ b/solution.py
@@ -2,6 +2,24 @@
 import jax.numpy as jnp
 from jax import lax
 from jax.sharding import PartitionSpec as P
+
+
+def ring_gather(array, axis, dim):
+    ways, here, step = (lax.axis_size(axis), lax.axis_index(axis), array.shape[dim])
+    shape = [n * ways if d == dim else n for d, n in enumerate(array.shape)]
+    full = lax.dynamic_update_slice_in_dim(
+        jnp.zeros(shape, array.dtype), array, here * step, axis=dim
+    )
+    going_up = going_down = array
+    for far in range(1, ways // 2 + 1):
+        going_up = lax.ppermute(going_up, axis, [(d, (d + 1) % ways) for d in range(ways)])
+        full = lax.dynamic_update_slice_in_dim(full, going_up, (here - far) % ways * step, axis=dim)
+        if 2 * far < ways:
+            going_down = lax.ppermute(going_down, axis, [(d, (d - 1) % ways) for d in range(ways)])
+            full = lax.dynamic_update_slice_in_dim(
+                full, going_down, (here + far) % ways * step, axis=dim
+            )
+    return full
 
 
 def partner(shard, axis, stride):
@@ -27,7 +45,7 @@
     owns_panel = col_index == row_index // per_column
 
     def gather(tile):
-        return lax.all_gather(tile, "row", axis=0, tiled=True)
+        return ring_gather(tile, "row", 0)
 
     def left_of(full):
         mine = lax.dynamic_slice_in_dim(full, offset, tile_rows, 1)

time: 416 us -> 368 us (0.88)
  waiting for transfers between devices: 360 us -> 213 us
  starting transfers between devices: 1.56 us -> 79.8 us
  local copies, waits for them, and re-layouts: 5.75 us -> 30 us
    all_gather x4 -> x0, waiting for transfers between devices: 320 us -> none  [gather(): return lax.all_gather(tile, 'row', axis=0, tiled=True)]
    ppermute x0 -> x12, waiting for transfers between devices: none -> 172 us  [the longest x8 151 us: ring_gather(): lax.ppermute(going_up, axis, [(d, (d + 1) % ways) for d in range(ways)])]
    ppermute x0 -> x12, starting transfers between devices: none -> 78.4 us  [the longest x8 72 us: ring_gather(): lax.ppermute(going_up, axis, [(d, (d + 1) % ways) for d in range(ways)])]
    dynamic_update_slice x0 -> x15, local copies, waits for them, and re-layouts: none -> 20.6 us  [the longest x8 12.1 us: ring_gather(): lax.dynamic_update_slice_in_dim(full, going_up, (here - far) % ways * ste...]
    another operation x0 -> x4, local copies, waits for them, and re-layouts: none -> 6.1 us
  transfers between devices with their start and end apart: 9 -> 17, of which waited for: 7 -> 12; matrix products, arithmetic and copies ran while one was open for 5% -> 12% of each run, Pallas kernels for 0% -> 0%
where the time goes in v1:
time: 368 us; the launch traced here: 367 us
  waiting for transfers between devices  213 us (58%)
  starting transfers between devices  79.8 us (22%)
  local copies, waits for them, and re-layouts  30 us (8%)
  matrix products  29.7 us (8%)
  between operations  13.6 us (4%)
    ppermute x8, waiting for transfers between devices, ring_gather(): lax.ppermute(going_up, axis, [(d, (d + 1) % ways) for d in range(ways)])  151 us
    ppermute x8, starting transfers between devices, ring_gather(): lax.ppermute(going_up, axis, [(d, (d + 1) % ways) for d in range(ways)])  72 us
    ppermute x1, waiting for transfers between devices, passed_along(): lax.ppermute(value, axis, [(source, source + steps) for source in range(f...  25.9 us
    ppermute x4, waiting for transfers between devices, ring_gather(): lax.ppermute(going_down, axis, [(d, (d - 1) % ways) for d in range(ways)])  20.8 us
    dot_general x3, matrix products, cross(): lax.dot_general(left, full, (((0,), (0,)), ((), ())), preferred_element_t...  15.5 us
    all_gather x2, waiting for transfers between devices, local(): whole = lax.all_gather(half, 'col', axis=1, tiled=True)  14.7 us
    dot_general x2, matrix products, local(): jnp.dot(whole, factor, preferred_element_type=jnp.float32)  14.2 us
    dynamic_update_slice x8, local copies, waits for them, and re-layouts, ring_gather(): lax.dynamic_update_slice_in_dim(full, going_up, (here - far) % ways * ste...  12.1 us
  transfers between devices with their start and end apart: 17, of which 12 were waited for; matrix products, arithmetic and copies ran while one was open for 12% of the time, Pallas kernels for 0%

profile of v1, /device:TPU:0, one launch (start us, length us, event | category | flops | bytes accessed | tf_op | source)
XLA Modules:
  0.0 367.3 jit_solution(16026790897290025642)
XLA Ops:
  6.5 3.0 collective-permute-start.4
  9.6 2.0 collective-permute-start.5
  11.6 24.3 %collective-permute-done.4 = bf16[512,1024]{1,0:T(8,128)(2,1)} collective-permute-done((bf16[512,1024]{1,0:T(8,128)(2,1)}, bf16[512,1024]{1,0:T(8,128)(2,1)}, u32[]{:S(2)}, u32[]{:S(2)}) %collective-permute-start.4) | collective-permute-done | bytes 1048608 | tf_op jit(solution)/shard_map/ppermute | solution.py:15
  35.9 21.8 %collective-permute-start = (bf16[512,1024]{1,0:T(8,128)(2,1)}, bf16[512,1024]{1,0:T(8,128)(2,1)}, u32[]{:S(2)}, u32[]{:S(2)}) collective-permute-start(bf16[512,1024]{1,0:T(8,128)(2,1)} %bitcast), channel_id=1, source_target_pairs={{0,2},{2,4},{4,6},{6,0},{1,3},{3,5},{5,7},{7,1},{8,10},{10,12},{12... | collective-permute-start | bytes 3145736 | tf_op jit(solution)/shard_map/ppermute | solution.py:15
  57.7 2.5 broadcast.8.clone.1
  60.2 1.4 constant_dynamic-update-slice_fusion.7
  61.6 1.6 collective-permute-start.8
  63.2 0.5 broadcast.8.clone.2
  63.8 0.1 constant_dynamic-update-slice_fusion.11
  63.9 1.3 constant_dynamic-update-slice_fusion.10
  65.2 1.3 constant_dynamic-update-slice_fusion.9
  66.6 16.1 %collective-permute-done.6 = bf16[512,1024]{1,0:T(8,128)(2,1)} collective-permute-done((bf16[512,1024]{1,0:T(8,128)(2,1)}, bf16[512,1024]{1,0:T(8,128)(2,1)}, u32[]{:S(2)}, u32[]{:S(2)}) %collective-permute-start.6) | collective-permute-done | bytes 1048608 | tf_op jit(solution)/shard_map/ppermute | solution.py:15
  82.7 1.3 constant_dynamic-update-slice_fusion.8
  84.0 0.2 constant_dynamic-slice_fusion
  84.4 2.1 collective-permute-start.1
  86.5 0.3 collective-permute-start.9
  86.8 18.6 %collective-permute-done = bf16[512,1024]{1,0:T(8,128)(2,1)} collective-permute-done((bf16[512,1024]{1,0:T(8,128)(2,1)}, bf16[512,1024]{1,0:T(8,128)(2,1)}, u32[]{:S(2)}, u32[]{:S(2)}) %collective-permute-start) | collective-permute-done | bytes 1048608 | tf_op jit(solution)/shard_map/ppermute | solution.py:15
  105.4 22.4 %collective-permute-done.8 = bf16[512,1024]{1,0:T(8,128)(2,1)} collective-permute-done((bf16[512,1024]{1,0:T(8,128)(2,1)S(1)}, bf16[512,1024]{1,0:T(8,128)(2,1)}, u32[]{:S(2)}, u32[]{:S(2)}) %collective-permute-start.8) | collective-permute-done | bytes 1048608 | tf_op jit(solution)/shard_map/ppermute | solution.py:15
  127.7 43.7 %collective-permute-start.10 = (bf16[512,1024]{1,0:T(8,128)(2,1)}, bf16[512,1024]{1,0:T(8,128)(2,1)}, u32[]{:S(2)}, u32[]{:S(2)}) collective-permute-start(bf16[512,1024]{1,0:T(8,128)(2,1)} %collective-permute-done.8), channel_id=1, source_target_pairs={{0,2},{2,4},{4,6},{6,0},{1,3},{3,5},{5,7},{7,1},{8,10},{10,12},{12... | collective-permute-start | bytes 3145736 | tf_op jit(solution)/shard_map/ppermute | solution.py:15
  171.4 2.5 broadcast.8.clone
  174.0 2.3 constant_dynamic-update-slice_fusion.15
  176.3 2.4 constant_dynamic-update-slice_fusion.14
  178.6 2.3 constant_dynamic-update-slice_fusion.6
  180.9 2.3 constant_dynamic-update-slice_fusion.13
  183.2 2.3 constant_dynamic-update-slice_fusion.5
  185.5 9.6 %collective-permute-done.2 = bf16[512,1024]{1,0:T(8,128)(2,1)} collective-permute-done((bf16[512,1024]{1,0:T(8,128)(2,1)}, bf16[512,1024]{1,0:T(8,128)(2,1)}, u32[]{:S(2)}, u32[]{:S(2)}) %collective-permute-start.2) | collective-permute-done | bytes 1048608 | tf_op jit(solution)/shard_map/ppermute | solution.py:15
  195.1 2.3 constant_dynamic-update-slice_fusion.12
  197.4 3.0 constant_dynamic-slice_fusion.1
  200.4 14.5 %collective-permute-done.10 = bf16[512,1024]{1,0:T(8,128)(2,1)} collective-permute-done((bf16[512,1024]{1,0:T(8,128)(2,1)}, bf16[512,1024]{1,0:T(8,128)(2,1)}, u32[]{:S(2)}, u32[]{:S(2)}) %collective-permute-start.10) | collective-permute-done | bytes 1048608 | tf_op jit(solution)/shard_map/ppermute | solution.py:15
  215.0 2.3 constant_dynamic-update-slice_fusion.4
  217.2 5.6 %convolution_convert_fusion.1 = bf16[512,1024]{1,0:T(8,128)(2,1)} fusion(bf16[2048,1024]{1,0:T(8,128)(2,1)} %constant_dynamic-update-slice_fusion.4, bf16[2048,512]{1,0:T(8,128)(2,1)S(1)} %constant_dynamic-slice_fusion, bf16[2048,512]{1,0:T(8,128)(2,1)} %collective-permute-done.7, pred[]{:T(512)S(6)} %eq.21), kind=kOutput, calls=%fused_computation.7 | convolution fusion | flops 2149056512 | bytes 9437185 | tf_op jit(solution)/shard_map/dot_general | solution.py:55
  222.9 6.6 %fusion = f32[512,1024]{1,0:T(8,128)} fusion(bf16[2048,1024]{1,0:T(8,128)(2,1)} %constant_dynamic-update-slice_fusion.12, bf16[2048,512]{1,0:T(8,128)(2,1)} %constant_dynamic-slice_fusion.1, bf16[2048,512]{1,0:T(8,128)(2,1)} %collective-permute-done.3, pred[]{:T(512)S(6)} %eq.21), kind=kOutput, calls=%fused_computation.1 | convolution fusion | flops 2148532224 | bytes 10485761 | tf_op jit(solution)/shard_map/dot_general | solution.py:55
  229.5 4.0 %all-gather.3.cloned.1.call-done = bf16[512,2048]{1,0:T(8,128)(2,1)} async-done(((bf16[512,1024]{1,0:T(8,128)(2,1)}), bf16[512,2048]{1,0:T(8,128)(2,1)}) %all-gather.3.cloned.1.call-update) | async-done | bytes 2097168 | tf_op jit(solution)/shard_map/all_gather | solution.py:68
  233.4 7.1 %fusion.3 = (bf16[512,1024]{1,0:T(8,128)(2,1)S(1)}, f32[512,1024]{1,0:T(8,128)}) fusion(f32[512,1024]{1,0:T(8,128)} %fusion, bf16[512,2048]{1,0:T(8,128)(2,1)} %all-gather.3.cloned.1.call-done, bf16[2048,1024]{1,0:T(8,128)(2,1)} %copy-done), kind=kOutput, calls=%fused_computation.26 | convolution fusion | flops 2148532224 | bytes 11534336 | tf_op jit(solution)/shard_map/dot_general | solution.py:69
  240.6 1.3 collective-permute-start.11
  241.9 25.9 %collective-permute-done.11 = bf16[512,1024]{1,0:T(8,128)(2,1)S(1)} collective-permute-done((bf16[512,1024]{1,0:T(8,128)(2,1)S(1)}, bf16[512,1024]{1,0:T(8,128)(2,1)S(1)}, u32[]{:S(2)}, u32[]{:S(2)}) %collective-permute-start.11) | collective-permute-done | bytes 1048608 | tf_op jit(solution)/shard_map/ppermute | solution.py:32
  267.7 1.8 collective-permute-start.12
  269.6 2.0 collective-permute-start.13
  271.6 24.1 %collective-permute-done.12 = bf16[512,1024]{1,0:T(8,128)(2,1)S(1)} collective-permute-done((bf16[512,1024]{1,0:T(8,128)(2,1)S(1)}, bf16[512,1024]{1,0:T(8,128)(2,1)S(1)}, u32[]{:S(2)}, u32[]{:S(2)}) %collective-permute-start.12) | collective-permute-done | bytes 1048608 | tf_op jit(solution)/shard_map/ppermute | solution.py:15
  295.7 0.5 broadcast.8
  296.2 0.1 constant_dynamic-update-slice_fusion.3
  296.3 0.1 constant_dynamic-update-slice_fusion.2
  296.4 20.8 %collective-permute-done.13 = bf16[512,1024]{1,0:T(8,128)(2,1)S(1)} collective-permute-done((bf16[512,1024]{1,0:T(8,128)(2,1)S(1)}, bf16[512,1024]{1,0:T(8,128)(2,1)S(1)}, u32[]{:S(2)}, u32[]{:S(2)}) %collective-permute-start.13) | collective-permute-done | bytes 1048608 | tf_op jit(solution)/shard_map/ppermute | solution.py:18
  317.3 0.1 constant_dynamic-update-slice_fusion.1
  317.4 21.8 %collective-permute-done.14 = bf16[512,1024]{1,0:T(8,128)(2,1)S(1)} collective-permute-done((bf16[512,1024]{1,0:T(8,128)(2,1)S(1)}, bf16[512,1024]{1,0:T(8,128)(2,1)S(1)}, u32[]{:S(2)}, u32[]{:S(2)}) %collective-permute-start.14) | collective-permute-done | bytes 1048608 | tf_op jit(solution)/shard_map/ppermute | solution.py:15
  339.3 3.3 convolution_convert_fusion
  342.7 10.7 %all-gather.5.cloned.1.call-done = bf16[512,2048]{1,0:T(8,128)(2,1)} async-done(((bf16[512,1024]{1,0:T(8,128)(2,1)}), bf16[512,2048]{1,0:T(8,128)(2,1)}) %all-gather.5.cloned.1.call-update) | async-done | bytes 2097168 | tf_op jit(solution)/shard_map/all_gather | solution.py:68
  353.4 7.1 %select_bitcast_fusion = f32[1,512,1024]{2,1,0:T(8,128)} fusion(f32[512,1024]{1,0:T(8,128)} %get-tuple-element.8, f32[512,1024]{1,0:T(8,128)} %fusion, bf16[512,2048]{1,0:T(8,128)(2,1)} %all-gather.5.cloned.1.call-done, bf16[2048,1024]{1,0:T(8,128)(2,1)} %copy-done, pred[]{:T(512)S(6)} %eq.20), kind=kOutput, calls=%fused_computation | convolution fusion | flops 2148532224 | bytes 12582913 | tf_op jit(solution)/shard_map/dot_general | solution.py:69
  (21 shorter events, 0.3 us)
Async XLA Ops:
  6.5 53.7 %copy-start.1 = (f32[512,1024]{1,0:T(8,128)S(1)}, f32[512,1024]{1,0:T(8,128)}, u32[]{:S(2)}) copy-start(f32[512,1024]{1,0:T(8,128)} %param.5) | copy-start | bytes 6291460
  6.5 226.9 %all-gather.3.cloned.1.call-start = ((), (), s32[]{:S(2)}) async-start(), calls=%async_computation | async-start | bytes 3145728 | tf_op jit(solution)/shard_map/all_gather | solution.py:68
  6.5 29.4 %collective-permute-start.4 = (bf16[512,1024]{1,0:T(8,128)(2,1)}, bf16[512,1024]{1,0:T(8,128)(2,1)}, u32[]{:S(2)}, u32[]{:S(2)}) collective-permute-start(bf16[512,1024]{1,0:T(8,128)(2,1)} %bitcast.13), channel_id=1, source_target_pairs={{0,2},{2,4},{4,6},{6,0},{1,3},{3,5},{5,7},{7,1},{8,10},{10,12},{12... | collective-permute-start | bytes 3145736 | tf_op jit(solution)/shard_map/ppermute | solution.py:15
  9.6 55.7 %collective-permute-start.5 = (bf16[512,1024]{1,0:T(8,128)(2,1)}, bf16[512,1024]{1,0:T(8,128)(2,1)}, u32[]{:S(2)}, u32[]{:S(2)}) collective-permute-start(bf16[512,1024]{1,0:T(8,128)(2,1)} %bitcast.14), channel_id=1, source_target_pairs={{0,6},{2,0},{4,2},{6,4},{1,7},{3,1},{5,3},{7,5},{8,14},{10,8},{12,... | collective-permute-start | bytes 3145736 | tf_op jit(solution)/shard_map/ppermute | solution.py:18
  35.9 46.8 %collective-permute-start.6 = (bf16[512,1024]{1,0:T(8,128)(2,1)}, bf16[512,1024]{1,0:T(8,128)(2,1)}, u32[]{:S(2)}, u32[]{:S(2)}) collective-permute-start(bf16[512,1024]{1,0:T(8,128)(2,1)} %collective-permute-done.4), channel_id=1, source_target_pairs={{0,2},{2,4},{4,6},{6,0},{1,3},{3,5},{5,7},{7,1},{8,10},{10,12},{12... | collective-permute-start | bytes 3145736 | tf_op jit(solution)/shard_map/ppermute | solution.py:15
  35.9 69.4 %collective-permute-start = (bf16[512,1024]{1,0:T(8,128)(2,1)}, bf16[512,1024]{1,0:T(8,128)(2,1)}, u32[]{:S(2)}, u32[]{:S(2)}) collective-permute-start(bf16[512,1024]{1,0:T(8,128)(2,1)} %bitcast), channel_id=1, source_target_pairs={{0,2},{2,4},{4,6},{6,0},{1,3},{3,5},{5,7},{7,1},{8,10},{10,12},{12... | collective-permute-start | bytes 3145736 | tf_op jit(solution)/shard_map/ppermute | solution.py:15
  61.6 2.1 copy-start.2
  61.6 66.1 %collective-permute-start.8 = (bf16[512,1024]{1,0:T(8,128)(2,1)S(1)}, bf16[512,1024]{1,0:T(8,128)(2,1)}, u32[]{:S(2)}, u32[]{:S(2)}) collective-permute-start(bf16[512,1024]{1,0:T(8,128)(2,1)S(1)} %get-tuple-element.6), channel_id=1, source_target_pairs={{0,2},{2,4},{4,6},{6,0},{1,3},{3,5},{5,7},{7,1},{8,10},{10,12},{12... | collective-permute-start | bytes 3145736 | tf_op jit(solution)/shard_map/ppermute | solution.py:15
  84.0 90.0 %copy-start = (bf16[2048,1024]{1,0:T(8,128)(2,1)}, bf16[2048,1024]{1,0:T(8,128)(2,1)S(1)}, u32[]{:S(2)}) copy-start(bf16[2048,1024]{1,0:T(8,128)(2,1)S(1)} %constant_dynamic-update-slice_fusion.8) | copy-start | bytes 12582916
  84.3 132.9 %collective-permute-start.7 = (bf16[2048,512]{1,0:T(8,128)(2,1)S(1)}, bf16[2048,512]{1,0:T(8,128)(2,1)}, u32[]{:S(2)}, u32[]{:S(2)}) collective-permute-start(bf16[2048,512]{1,0:T(8,128)(2,1)S(1)} %constant_dynamic-slice_fusion), channel_id=1, source_target_pairs={{0,1},{1,0},{2,3},{3,2},{4,5},{5,4},{6,7},{7,6},{8,9},{9,8},{10,11... | collective-permute-start | bytes 6291464 | tf_op jit(solution)/shard_map/ppermute | solution.py:26
  84.4 96.6 %collective-permute-start.1 = (bf16[512,1024]{1,0:T(8,128)(2,1)}, bf16[512,1024]{1,0:T(8,128)(2,1)}, u32[]{:S(2)}, u32[]{:S(2)}) collective-permute-start(bf16[512,1024]{1,0:T(8,128)(2,1)} %bitcast), channel_id=1, source_target_pairs={{0,6},{2,0},{4,2},{6,4},{1,7},{3,1},{5,3},{7,5},{8,14},{10,8},{12,... | collective-permute-start | bytes 3145736 | tf_op jit(solution)/shard_map/ppermute | solution.py:18
  86.5 96.8 %collective-permute-start.9 = (bf16[512,1024]{1,0:T(8,128)(2,1)S(1)}, bf16[512,1024]{1,0:T(8,128)(2,1)}, u32[]{:S(2)}, u32[]{:S(2)}) collective-permute-start(bf16[512,1024]{1,0:T(8,128)(2,1)S(1)} %get-tuple-element.6), channel_id=1, source_target_pairs={{0,6},{2,0},{4,2},{6,4},{1,7},{3,1},{5,3},{7,5},{8,14},{10,8},{12,... | collective-permute-start | bytes 3145736 | tf_op jit(solution)/shard_map/ppermute | solution.py:18
  105.4 89.8 %collective-permute-start.2 = (bf16[512,1024]{1,0:T(8,128)(2,1)}, bf16[512,1024]{1,0:T(8,128)(2,1)}, u32[]{:S(2)}, u32[]{:S(2)}) collective-permute-start(bf16[512,1024]{1,0:T(8,128)(2,1)} %collective-permute-done), channel_id=1, source_target_pairs={{0,2},{2,4},{4,6},{6,0},{1,3},{3,5},{5,7},{7,1},{8,10},{10,12},{12... | collective-permute-start | bytes 3145736 | tf_op jit(solution)/shard_map/ppermute | solution.py:15
  127.7 87.2 %collective-permute-start.10 = (bf16[512,1024]{1,0:T(8,128)(2,1)}, bf16[512,1024]{1,0:T(8,128)(2,1)}, u32[]{:S(2)}, u32[]{:S(2)}) collective-permute-start(bf16[512,1024]{1,0:T(8,128)(2,1)} %collective-permute-done.8), channel_id=1, source_target_pairs={{0,2},{2,4},{4,6},{6,0},{1,3},{3,5},{5,7},{7,1},{8,10},{10,12},{12... | collective-permute-start | bytes 3145736 | tf_op jit(solution)/shard_map/ppermute | solution.py:15
  200.4 22.4 %collective-permute-start.3 = (bf16[2048,512]{1,0:T(8,128)(2,1)}, bf16[2048,512]{1,0:T(8,128)(2,1)}, u32[]{:S(2)}, u32[]{:S(2)}) collective-permute-start(bf16[2048,512]{1,0:T(8,128)(2,1)} %constant_dynamic-slice_fusion.1), channel_id=1, source_target_pairs={{0,1},{1,0},{2,3},{3,2},{4,5},{5,4},{6,7},{7,6},{8,9},{9,8},{10,11... | collective-permute-start | bytes 6291464 | tf_op jit(solution)/shard_map/ppermute | solution.py:26
  222.8 130.6 %all-gather.5.cloned.1.call-start = ((), (), s32[]{:S(2)}) async-start(), calls=%async_computation.1 | async-start | bytes 3145728 | tf_op jit(solution)/shard_map/all_gather | solution.py:68
  240.6 27.2 %collective-permute-start.11 = (bf16[512,1024]{1,0:T(8,128)(2,1)S(1)}, bf16[512,1024]{1,0:T(8,128)(2,1)S(1)}, u32[]{:S(2)}, u32[]{:S(2)}) collective-permute-start(bf16[512,1024]{1,0:T(8,128)(2,1)S(1)} %get-tuple-element.7), channel_id=1, source_target_pairs={{8,0},{9,1},{10,2},{11,3},{12,4},{13,5},{14,6},{15,7},{24,16},{25,... | collective-permute-start | bytes 3145736 | tf_op jit(solution)/shard_map/ppermute | solution.py:32
  267.7 27.9 %collective-permute-start.12 = (bf16[512,1024]{1,0:T(8,128)(2,1)S(1)}, bf16[512,1024]{1,0:T(8,128)(2,1)S(1)}, u32[]{:S(2)}, u32[]{:S(2)}) collective-permute-start(bf16[512,1024]{1,0:T(8,128)(2,1)S(1)} %collective-permute-done.11), channel_id=1, source_target_pairs={{0,2},{2,4},{4,6},{6,0},{1,3},{3,5},{5,7},{7,1},{8,10},{10,12},{12... | collective-permute-start | bytes 3145736 | tf_op jit(solution)/shard_map/ppermute | solution.py:15
  269.6 47.7 %collective-permute-start.13 = (bf16[512,1024]{1,0:T(8,128)(2,1)S(1)}, bf16[512,1024]{1,0:T(8,128)(2,1)S(1)}, u32[]{:S(2)}, u32[]{:S(2)}) collective-permute-start(bf16[512,1024]{1,0:T(8,128)(2,1)S(1)} %collective-permute-done.11), channel_id=1, source_target_pairs={{0,6},{2,0},{4,2},{6,4},{1,7},{3,1},{5,3},{7,5},{8,14},{10,8},{12,... | collective-permute-start | bytes 3145736 | tf_op jit(solution)/shard_map/ppermute | solution.py:18
  295.6 43.6 %collective-permute-start.14 = (bf16[512,1024]{1,0:T(8,128)(2,1)S(1)}, bf16[512,1024]{1,0:T(8,128)(2,1)S(1)}, u32[]{:S(2)}, u32[]{:S(2)}) collective-permute-start(bf16[512,1024]{1,0:T(8,128)(2,1)S(1)} %collective-permute-done.12), channel_id=1, source_target_pairs={{0,2},{2,4},{4,6},{6,0},{1,3},{3,5},{5,7},{7,1},{8,10},{10,12},{12... | collective-permute-start | bytes 3145736 | tf_op jit(solution)/shard_map/ppermute | solution.py:15
Sparse Core Ops, SparseCore 0:
  222.9 10.4 all-gather.2
  342.8 10.5 all-gather.4
